TPU v7x, 128 devices: a whole 4x4x4 slice. The times are simulated.
128 devices in a mesh: sx: 16 (over z, y), sy: 8 (over x, core).
Axes of the slice: x: 4, y: 4, z: 4, core: 2. Of those that a mesh axis runs over, the one named last changes fastest.
Arguments:
- obs_values: bfloat16 [32768, 64], P(('sx', 'sy')), may hold values from -6 to 6
- obs_dest: int32 [32768, 1], P(('sx', 'sy')), may hold values from 0 to 127; in each aligned block of 256 rows (0 to 255, 256 to 511, ...) at most 4 rows name the same one
- obs_node: int32 [32768], P(('sx', 'sy')), may hold values from 0 to 2047
- schur: bfloat16 [16, 8, 2048, 2048], P('sx', 'sy'), as said below
- local_inverse: bfloat16 [16, 8, 2048, 2048], P('sx', 'sy'), as said below
- coarse_inverse: float32 [1024, 1024], P(('sx', 'sy')), as said below
Outputs:
- solution_field: float32 [16, 8, 64, 2048], P('sx', 'sy')
- residual: float32 [16, 8, 64, 2048], P('sx', 'sy')
Inputs may be any that keep to these rules, and one draw needn't show every extreme that they name: `obs_dest`: at most 4 observations of one device go to one subdomain. `schur`: symmetric positive definite. `local_inverse`: symmetric positive definite. `coarse_inverse`: symmetric positive definite.
All inputs are finite; a program needn't handle non-finite values.
Results may differ from a plain program's by a relative error of at most 0.04.
Values may be sent and summed in bfloat16 or wider, within the bound.
A program may use at most 128 MiB of HBM per device.

v0:
```python
import jax
import jax.numpy as jnp
from jax import lax
from jax.sharding import PartitionSpec as P

ITERS = 6


def shortened(array):

    def short(part):
        return part.astype(jnp.bfloat16) if part.dtype == jnp.float32 else part

    return jax.tree.map(short, array)


def padded_2(cells, sides, width):
    for axis, dim in sides:
        count = lax.axis_size(axis)
        ends = count - 1
        head = lax.slice_in_dim(cells, 0, width, axis=dim)
        tail = lax.slice_in_dim(cells, cells.shape[dim] - width, cells.shape[dim], axis=dim)
        cells = jnp.concatenate(
            [
                lax.ppermute(tail, axis, [(i, (i + 1) % count) for i in range(ends)]),
                cells,
                lax.ppermute(head, axis, [((i + 1) % count, i) for i in range(ends)]),
            ],
            axis=dim,
        )
    return cells


def edge_weights(size):
    edge_len = size // 4
    col_index = lax.axis_index("sx")
    row_index = lax.axis_index("sy")
    col_count = lax.axis_size("sx")
    row_count = lax.axis_size("sy")
    sides = (
        jnp.where(col_index > 0, 0.5, 1.0),
        jnp.where(col_index < col_count - 1, 0.5, 1.0),
        jnp.where(row_index > 0, 0.5, 1.0),
        jnp.where(row_index < row_count - 1, 0.5, 1.0),
    )
    return jnp.concatenate([jnp.full((edge_len,), value, jnp.float32) for value in sides])


def coarse_basis(size, count):
    edge_len = size // 4
    node = jnp.arange(size)
    side = node // edge_len
    offset = (node % edge_len).astype(jnp.float32) - (edge_len - 1) / 2.0
    norm_ramp = jnp.sqrt(jnp.float32(edge_len * (edge_len * edge_len - 1) / 12.0))
    column = jnp.arange(count)
    on_edge = side[:, None] == (column // 2)[None, :]
    value = jnp.where(
        (column % 2 == 0)[None, :],
        1.0 / jnp.sqrt(jnp.float32(edge_len)),
        offset[:, None] / norm_ramp,
    )
    return jnp.where(on_edge, value, 0.0)


def assemble(local):
    edge_len = local.shape[1] // 4
    west_part = local[:, 0:edge_len]
    east_part = local[:, edge_len : 2 * edge_len]
    south_part = local[:, 2 * edge_len : 3 * edge_len]
    north_part = local[:, 3 * edge_len :]
    padded = padded_2(shortened(local[None, None]), (("sx", 0), ("sy", 1)), 1)
    west = west_part + padded[0, 1, :, edge_len : 2 * edge_len]
    east = east_part + padded[2, 1, :, 0:edge_len]
    south = south_part + padded[1, 0, :, 3 * edge_len :]
    north = north_part + padded[1, 2, :, 2 * edge_len : 3 * edge_len]
    return jnp.concatenate([west, east, south, north], axis=1)


def gather_coarse(coarse_local):
    return lax.all_gather(coarse_local, ("sx", "sy"), axis=0, tiled=True)


def body(obs_values, obs_dest, obs_node, schur, local_inverse, coarse_inverse):
    hp = lax.Precision.HIGHEST
    size = schur.shape[-1]
    count = coarse_inverse.shape[0]
    realiz = obs_values.shape[1]
    obs_count = obs_values.shape[0]
    row_count = lax.axis_size("sy")
    dev_count = lax.axis_size("sx") * row_count
    target = obs_dest[:, 0]
    capacity = max(2, 2 * obs_count // dev_count)
    match_table = (target[:, None] == jnp.arange(dev_count)[None, :]).astype(jnp.int32)
    slot_index = jnp.sum(jnp.cumsum(match_table, axis=0) * match_table, axis=1) - 1
    position = target * capacity + slot_index
    send_values = (
        jnp.zeros((dev_count * capacity, realiz), jnp.bfloat16).at[position].set(obs_values)
    )
    send_nodes = jnp.zeros((dev_count * capacity,), jnp.int32).at[position].set(obs_node)
    got_values, got_nodes = (
        lax.all_to_all(
            send_values.reshape(dev_count, capacity, realiz),
            ("sx", "sy"),
            split_axis=0,
            concat_axis=0,
            tiled=True,
        ),
        lax.all_to_all(
            send_nodes.reshape(dev_count, capacity),
            ("sx", "sy"),
            split_axis=0,
            concat_axis=0,
            tiled=True,
        ),
    )
    load = jax.ops.segment_sum(
        got_values.reshape(-1, realiz).astype(jnp.float32), got_nodes.reshape(-1), num_segments=size
    )
    rhs = assemble(load.T)
    weight = edge_weights(size)[None, :]
    basis = coarse_basis(size, count)
    schur_mat = schur[0, 0]
    inverse_mat = local_inverse[0, 0]

    def project(vec):
        return jnp.dot(weight * vec, basis, precision=hp).T

    def precond(vec, coarse_all):
        scaled = weight * vec
        part = jnp.dot(scaled.astype(jnp.bfloat16), inverse_mat, preferred_element_type=jnp.float32)
        solved = jnp.dot(coarse_inverse, coarse_all, precision=hp)
        correction = jnp.dot(solved.T, basis.T, precision=hp)
        return assemble(weight * (part + correction))

    def products(left, right):
        return lax.psum(jnp.sum(weight * left * right, axis=1), ("sx", "sy"))

    solution_field = jnp.zeros_like(rhs)
    residual = rhs
    coarse_resid = gather_coarse(project(residual))
    precon = precond(residual, coarse_resid)
    direction = precon
    rz_now = products(residual, precon)
    for step in range(ITERS):
        image = assemble(
            jnp.dot(direction.astype(jnp.bfloat16), schur_mat, preferred_element_type=jnp.float32)
        )
        curv_local = jnp.sum(weight * direction * image, axis=1)
        curv = lax.psum(curv_local, ("sx", "sy"))
        alpha = rz_now / curv
        solution_field = solution_field + alpha[:, None] * direction
        residual = residual - alpha[:, None] * image
        if step < ITERS - 1:
            coarse_resid = gather_coarse(project(residual))
            precon = precond(residual, coarse_resid)
            rz_next = products(residual, precon)
            direction = precon + (rz_next / rz_now)[:, None] * direction
            rz_now = rz_next
    return (solution_field[None, None], residual[None, None])


def solution(mesh):
    placed = (
        P(("sx", "sy"), None),
        P(("sx", "sy"), None),
        P(("sx", "sy")),
        P("sx", "sy", None, None),
        P("sx", "sy", None, None),
        P(("sx", "sy"), None),
    )
    return jax.shard_map(
        body,
        mesh=mesh,
        in_specs=placed,
        out_specs=(P("sx", "sy", None, None), P("sx", "sy", None, None)),
        check_vma=False,
    )
```

profile of v0, /device:TPU:1, one launch (start us, length us, event | category | flops | bytes accessed | tf_op | source)
XLA Modules:
  0.0 1432.0 jit_solution(6117860953516433841)
XLA Ops:
  5.6 11.5 all-to-all-start
  32.6 8.1 all-to-all-done.1
  60.7 7.6 collective-permute-done.3
  72.7 39.9 %all_gather.18 = f32[1024,64]{1,0:T(8,128)S(1)} all-gather(f32[8,64]{1,0:T(8,128)S(1)} %fusion.35), channel_id=1, replica_groups=mesh['sx'=16,'sy'=8] {'sx','sy'}, dimensions={0}, use_global_device_ids=true | all-gather | bytes 264192 | tf_op jit(solution)/shard_map/all_gather | solution.py:80
  136.0 7.7 collective-permute-done.7
  163.3 7.7 collective-permute-done.11
  172.5 69.8 %all-reduce = (f32[64]{0:T(128)S(1)}, f32[64]{0:T(128)S(1)}) all-reduce(f32[64]{0:T(128)S(1)} %get-tuple-element.3, f32[64]{0:T(128)S(1)} %get-tuple-element.2), channel_id=1, replica_groups=mesh['sx'=16,'sy'=8] {'sx','sy'}, use_global_device_ids=true, to_apply=%region_7.8 | all-reduce | flops 128 | bytes 1024 | tf_op jit(solution)/shard_map/psum | solution.py:136
  249.8 34.5 %all_gather.19 = f32[1024,64]{1,0:T(8,128)S(1)} all-gather(f32[8,64]{1,0:T(8,128)S(1)} %fusion.34), channel_id=1, replica_groups=mesh['sx'=16,'sy'=8] {'sx','sy'}, dimensions={0}, use_global_device_ids=true | all-gather | bytes 264192 | tf_op jit(solution)/shard_map/all_gather | solution.py:80
  302.5 7.7 collective-permute-done.15
  311.7 67.8 %psum.86 = f32[64]{0:T(128)S(1)} all-reduce(f32[64]{0:T(128)S(1)} %multiply_reduce_fusion.8), channel_id=1, replica_groups=mesh['sx'=16,'sy'=8] {'sx','sy'}, use_global_device_ids=true, to_apply=%region_11.12 | all-reduce | flops 64 | bytes 512 | tf_op jit(solution)/shard_map/psum | solution.py:136
  400.4 7.4 collective-permute-done.19
  409.6 68.1 %psum.87 = f32[64]{0:T(128)S(1)} all-reduce(f32[64]{0:T(128)S(1)} %multiply_reduce_fusion.7), channel_id=1, replica_groups=mesh['sx'=16,'sy'=8] {'sx','sy'}, use_global_device_ids=true, to_apply=%region_13.14 | all-reduce | flops 64 | bytes 512 | tf_op jit(solution)/shard_map/psum | solution.py:149
  485.2 34.6 %all_gather.20 = f32[1024,64]{1,0:T(8,128)S(1)} all-gather(f32[8,64]{1,0:T(8,128)S(1)} %fusion.33), channel_id=1, replica_groups=mesh['sx'=16,'sy'=8] {'sx','sy'}, dimensions={0}, use_global_device_ids=true | all-gather | bytes 264192 | tf_op jit(solution)/shard_map/all_gather | solution.py:80
  538.0 7.7 collective-permute-done.23
  547.9 68.0 %psum.88 = f32[64]{0:T(128)S(1)} all-reduce(f32[64]{0:T(128)S(1)} %multiply_reduce_fusion.6), channel_id=1, replica_groups=mesh['sx'=16,'sy'=8] {'sx','sy'}, use_global_device_ids=true, to_apply=%region_15.16 | all-reduce | flops 64 | bytes 512 | tf_op jit(solution)/shard_map/psum | solution.py:136
  637.8 7.3 collective-permute-done.27
  647.0 68.1 %psum.89 = f32[64]{0:T(128)S(1)} all-reduce(f32[64]{0:T(128)S(1)} %multiply_reduce_fusion.5), channel_id=1, replica_groups=mesh['sx'=16,'sy'=8] {'sx','sy'}, use_global_device_ids=true, to_apply=%region_17.18 | all-reduce | flops 64 | bytes 512 | tf_op jit(solution)/shard_map/psum | solution.py:149
  723.6 34.8 %all_gather.21 = f32[1024,64]{1,0:T(8,128)S(1)} all-gather(f32[8,64]{1,0:T(8,128)S(1)} %fusion.32), channel_id=1, replica_groups=mesh['sx'=16,'sy'=8] {'sx','sy'}, dimensions={0}, use_global_device_ids=true | all-gather | bytes 264192 | tf_op jit(solution)/shard_map/all_gather | solution.py:80
  776.6 7.7 collective-permute-done.31
  785.8 68.0 %psum.90 = f32[64]{0:T(128)S(1)} all-reduce(f32[64]{0:T(128)S(1)} %multiply_reduce_fusion.4), channel_id=1, replica_groups=mesh['sx'=16,'sy'=8] {'sx','sy'}, use_global_device_ids=true, to_apply=%region_19.20 | all-reduce | flops 64 | bytes 512 | tf_op jit(solution)/shard_map/psum | solution.py:136
  874.7 7.3 collective-permute-done.35
  883.9 68.1 %psum.91 = f32[64]{0:T(128)S(1)} all-reduce(f32[64]{0:T(128)S(1)} %multiply_reduce_fusion.3), channel_id=1, replica_groups=mesh['sx'=16,'sy'=8] {'sx','sy'}, use_global_device_ids=true, to_apply=%region_21.22 | all-reduce | flops 64 | bytes 512 | tf_op jit(solution)/shard_map/psum | solution.py:149
  959.4 34.5 %all_gather.22 = f32[1024,64]{1,0:T(8,128)S(1)} all-gather(f32[8,64]{1,0:T(8,128)S(1)} %fusion.31), channel_id=1, replica_groups=mesh['sx'=16,'sy'=8] {'sx','sy'}, dimensions={0}, use_global_device_ids=true | all-gather | bytes 264192 | tf_op jit(solution)/shard_map/all_gather | solution.py:80
  1012.2 7.7 collective-permute-done.39
  1022.2 68.0 %psum.92 = f32[64]{0:T(128)S(1)} all-reduce(f32[64]{0:T(128)S(1)} %multiply_reduce_fusion.2), channel_id=1, replica_groups=mesh['sx'=16,'sy'=8] {'sx','sy'}, use_global_device_ids=true, to_apply=%region_23.24 | all-reduce | flops 64 | bytes 512 | tf_op jit(solution)/shard_map/psum | solution.py:136
  1112.1 7.3 collective-permute-done.43
  1121.3 68.1 %psum.93 = f32[64]{0:T(128)S(1)} all-reduce(f32[64]{0:T(128)S(1)} %multiply_reduce_fusion.1), channel_id=1, replica_groups=mesh['sx'=16,'sy'=8] {'sx','sy'}, use_global_device_ids=true, to_apply=%region_25.26 | all-reduce | flops 64 | bytes 512 | tf_op jit(solution)/shard_map/psum | solution.py:149
  1196.8 34.6 %all_gather.23 = f32[1024,64]{1,0:T(8,128)S(1)} all-gather(f32[8,64]{1,0:T(8,128)S(1)} %fusion.30), channel_id=1, replica_groups=mesh['sx'=16,'sy'=8] {'sx','sy'}, dimensions={0}, use_global_device_ids=true | all-gather | bytes 264192 | tf_op jit(solution)/shard_map/all_gather | solution.py:80
  1249.6 7.7 collective-permute-done.47
  1258.8 68.0 %psum.94 = f32[64]{0:T(128)S(1)} all-reduce(f32[64]{0:T(128)S(1)} %multiply_reduce_fusion), channel_id=1, replica_groups=mesh['sx'=16,'sy'=8] {'sx','sy'}, use_global_device_ids=true, to_apply=%region_27.28 | all-reduce | flops 64 | bytes 512 | tf_op jit(solution)/shard_map/psum | solution.py:136
  1347.6 7.3 collective-permute-done.51
  1357.7 68.1 %psum.95 = f32[64]{0:T(128)S(1)} all-reduce(f32[64]{0:T(128)S(1)} %fusion.48), channel_id=1, replica_groups=mesh['sx'=16,'sy'=8] {'sx','sy'}, use_global_device_ids=true, to_apply=%region_29.30 | all-reduce | flops 64 | bytes 512 | tf_op jit(solution)/shard_map/psum | solution.py:149
  (316 shorter events, 348.6 us)
Async XLA Ops:
  5.6 21.0 %all-to-all-start = ((s32[128,1,4]{2,1,0:T(1,128)}), s32[128,1,4]{2,1,0:T(1,128)S(1)}, u32[]{:S(2)}, u32[]{:S(2)}) async-start(s32[128,1,4]{2,1,0:T(1,128)} %bitcast.7), calls=%async_computation | async-start | bytes 131072 | tf_op jit(solution)/shard_map/all_to_all | solution.py:108
  26.6 14.0 all-to-all-start.1
  53.7 14.6 %collective-permute-start.3 = (bf16[3,1,64,2048]{3,2,1,0:T(8,128)(2,1)S(1)}, bf16[3,1,64,2048]{3,2,1,0:T(8,128)(2,1)S(1)}, u32[]{:S(2)}, u32[]{:S(2)}) collective-permute-start(bf16[3,1,64,2048]{3,2,1,0:T(8,128)(2,1)S(1)} %pad_maximum_fusion), channel_id=1, source_target_pairs={{1,0},{2,1},{3,2},{4,3},{5,4},{6,5},{7,6},{9,8},{10,9},{11,10},{12... | collective-permute-start | bytes 2359304 | tf_op jit(solution)/shard_map/ppermute | solution.py:27
  57.6 11.9 collective-permute-start.2
  119.8 9.6 collective-permute-start.5
  130.4 13.3 collective-permute-start.7
  133.6 11.3 collective-permute-start.6
  156.1 15.0 %collective-permute-start.11 = (bf16[3,1,64,2048]{3,2,1,0:T(8,128)(2,1)S(1)}, bf16[3,1,64,2048]{3,2,1,0:T(8,128)(2,1)S(1)}, u32[]{:S(2)}, u32[]{:S(2)}) collective-permute-start(bf16[3,1,64,2048]{3,2,1,0:T(8,128)(2,1)S(1)} %pad_maximum_fusion.2), channel_id=1, source_target_pairs={{1,0},{2,1},{3,2},{4,3},{5,4},{6,5},{7,6},{9,8},{10,9},{11,10},{12... | collective-permute-start | bytes 2359304 | tf_op jit(solution)/shard_map/ppermute | solution.py:27
  158.0 14.2 collective-permute-start.10
  286.4 9.6 collective-permute-start.13
  297.0 13.3 collective-permute-start.15
  300.2 11.3 collective-permute-start.14
  394.3 13.5 collective-permute-start.19
  398.5 10.8 collective-permute-start.18
  521.8 9.6 collective-permute-start.21
  532.4 13.3 collective-permute-start.23
  535.6 11.3 collective-permute-start.22
  631.7 13.4 collective-permute-start.27
  635.9 10.8 collective-permute-start.26
  771.0 13.3 collective-permute-start.31
  774.2 11.3 collective-permute-start.30
  868.5 13.4 collective-permute-start.35
  872.8 10.8 collective-permute-start.34
  996.0 9.6 collective-permute-start.37
  1006.6 13.3 collective-permute-start.39
  1009.8 11.3 collective-permute-start.38
  1106.0 13.4 collective-permute-start.43
  1110.2 10.8 collective-permute-start.42
  1244.0 13.3 collective-permute-start.47
  1247.2 11.3 collective-permute-start.46
  1341.5 13.5 collective-permute-start.51
  1345.7 10.8 collective-permute-start.50
  (67 other events, 2812.2 us)
where the time goes:
time: 1440 us; the launch traced here: 1430 us
  blocking collectives  963 us (67%)
  waiting for transfers between devices  190 us (13%)
  starting transfers between devices  164 us (11%)
  matrix products  82.1 us (6%)
  other arithmetic  20.9 us (1%)
    psum x6, blocking collectives, products(): return lax.psum(jnp.sum(weight * left * right, axis=1), ('sx', 'sy'))  410 us
    psum x5, blocking collectives, body(): curv = lax.psum(curv_local, ('sx', 'sy'))  340 us
    all_gather x6, blocking collectives, gather_coarse(): return lax.all_gather(coarse_local, ('sx', 'sy'), axis=0, tiled=True)  213 us
    ppermute x26, waiting for transfers between devices, padded_2(): lax.ppermute(head, axis, [((i + 1) % count, i) for i in range(ends)])  146 us
    ppermute x26, starting transfers between devices, padded_2(): lax.ppermute(tail, axis, [(i, (i + 1) % count) for i in range(ends)])  84.9 us
    ppermute x26, starting transfers between devices, padded_2(): lax.ppermute(head, axis, [((i + 1) % count, i) for i in range(ends)])  62.8 us
    dot_general x6, matrix products, precond(): jnp.dot(scaled.astype(jnp.bfloat16), inverse_mat, preferred_element_type=...  29.9 us
    ppermute x26, waiting for transfers between devices, padded_2(): lax.ppermute(tail, axis, [(i, (i + 1) % count) for i in range(ends)])  29.5 us
  transfers between devices with their start and end apart: 54, of which 54 were waited for; matrix products, arithmetic and copies ran while one was open for 0% of the time, Pallas kernels for 0%

commit v1 on v0

--- a/solution.py
+++ b/solution.py
@@ -1,9 +1,18 @@
+import functools
 import jax
 import jax.numpy as jnp
 from jax import lax
 from jax.sharding import PartitionSpec as P
 
 ITERS = 6
+
+
+def work_table_all(chunk, dim_at):
+    outcome_arr = lax.all_to_all(jnp.stack([chunk] * lax.psum(1, ("sx", "sy"))), ("sx", "sy"), 0, 0)
+    return jnp.concatenate(outcome_arr, axis=dim_at)
+
+
+feed_block = functools.partial(work_table_all, dim_at=0)
 
 
 def shortened(array):
@@ -77,7 +86,7 @@
 
 
 def gather_coarse(coarse_local):
-    return lax.all_gather(coarse_local, ("sx", "sy"), axis=0, tiled=True)
+    return feed_block(coarse_local)
 
 
 def body(obs_values, obs_dest, obs_node, schur, local_inverse, coarse_inverse):

time: 1440 us -> 1320 us (0.917)
  blocking collectives: 963 us -> 745 us
  starting transfers between devices: 164 us -> 205 us
  waiting for transfers between devices: 190 us -> 219 us
    all_gather x6 -> x0, blocking collectives: 213 us -> none  [gather_coarse(): return lax.all_gather(coarse_local, ('sx', 'sy'), axis=0, tiled=True)]
    all_to_all x0 -> x6, starting transfers between devices: none -> 39.6 us  [work_table_all(): lax.all_to_all(jnp.stack([chunk] * lax.psum(1, ('sx', 'sy'))), ('sx', 'sy...]
    all_to_all x0 -> x6, waiting for transfers between devices: none -> 32.4 us  [work_table_all(): lax.all_to_all(jnp.stack([chunk] * lax.psum(1, ('sx', 'sy'))), ('sx', 'sy...]
  transfers between devices with their start and end apart: 54 -> 60, of which waited for: 54 -> 60; matrix products, arithmetic and copies ran while one was open for 0% -> 3% of each run, Pallas kernels for 0% -> 0%
where the time goes in v1:
time: 1320 us; the launch traced here: 1310 us
  blocking collectives  745 us (56%)
  waiting for transfers between devices  219 us (17%)
  starting transfers between devices  205 us (16%)
  matrix products  94 us (7%)
  other arithmetic  28.3 us (2%)
  local copies, waits for them, and re-layouts  17.3 us (1%)
    psum x6, blocking collectives, products(): return lax.psum(jnp.sum(weight * left * right, axis=1), ('sx', 'sy'))  405 us
    psum x5, blocking collectives, body(): curv = lax.psum(curv_local, ('sx', 'sy'))  339 us
    ppermute x26, waiting for transfers between devices, padded_2(): lax.ppermute(head, axis, [((i + 1) % count, i) for i in range(ends)])  145 us
    ppermute x26, starting transfers between devices, padded_2(): lax.ppermute(tail, axis, [(i, (i + 1) % count) for i in range(ends)])  83.7 us
    ppermute x26, starting transfers between devices, padded_2(): lax.ppermute(head, axis, [((i + 1) % count, i) for i in range(ends)])  66.2 us
    all_to_all x6, starting transfers between devices, work_table_all(): lax.all_to_all(jnp.stack([chunk] * lax.psum(1, ('sx', 'sy'))), ('sx', 'sy...  39.6 us
    dot_general x6, matrix products, precond(): jnp.dot(scaled.astype(jnp.bfloat16), inverse_mat, preferred_element_type=...  32.9 us
    all_to_all x6, waiting for transfers between devices, work_table_all(): lax.all_to_all(jnp.stack([chunk] * lax.psum(1, ('sx', 'sy'))), ('sx', 'sy...  32.4 us
  transfers between devices with their start and end apart: 60, of which 60 were waited for; matrix products, arithmetic and copies ran while one was open for 3% of the time, Pallas kernels for 0%

profile of v1, /device:TPU:1, one launch (start us, length us, event | category | flops | bytes accessed | tf_op | source)
XLA Modules:
  0.0 1312.0 jit_solution(12134029944559749624)
XLA Ops:
  5.6 11.5 all-to-all-start
  19.9 6.7 all-to-all-done
  32.6 8.1 all-to-all-done.1
  60.7 7.6 collective-permute-done.3
  73.8 11.2 all-to-all-start.2
  90.0 5.9 all-to-all-done.2
  115.9 7.7 collective-permute-done.7
  146.8 7.7 collective-permute-done.11
  156.1 69.0 %all-reduce = (f32[64]{0:T(128)S(1)}, f32[64]{0:T(128)S(1)}) all-reduce(f32[64]{0:T(128)S(1)} %get-tuple-element.3, f32[64]{0:T(128)S(1)} %get-tuple-element.2), channel_id=1, replica_groups=mesh['sx'=16,'sy'=8] {'sx','sy'}, use_global_device_ids=true, to_apply=%region_7.8 | all-reduce | flops 128 | bytes 1024 | tf_op jit(solution)/shard_map/psum | solution.py:145
  239.1 5.9 all-to-all-done.3
  264.3 7.7 collective-permute-done.15
  273.5 67.2 %psum.86 = f32[64]{0:T(128)S(1)} all-reduce(f32[64]{0:T(128)S(1)} %multiply_reduce_fusion.8), channel_id=1, replica_groups=mesh['sx'=16,'sy'=8] {'sx','sy'}, use_global_device_ids=true, to_apply=%region_11.12 | all-reduce | flops 64 | bytes 512 | tf_op jit(solution)/shard_map/psum | solution.py:145
  361.6 7.7 collective-permute-done.19
  370.8 68.0 %psum.87 = f32[64]{0:T(128)S(1)} all-reduce(f32[64]{0:T(128)S(1)} %multiply_reduce_fusion.7), channel_id=1, replica_groups=mesh['sx'=16,'sy'=8] {'sx','sy'}, use_global_device_ids=true, to_apply=%region_13.14 | all-reduce | flops 64 | bytes 512 | tf_op jit(solution)/shard_map/psum | solution.py:158
  447.9 5.7 fusion.18
  479.5 7.7 collective-permute-done.23
  489.5 67.4 %psum.88 = f32[64]{0:T(128)S(1)} all-reduce(f32[64]{0:T(128)S(1)} %multiply_reduce_fusion.6), channel_id=1, replica_groups=mesh['sx'=16,'sy'=8] {'sx','sy'}, use_global_device_ids=true, to_apply=%region_15.16 | all-reduce | flops 64 | bytes 512 | tf_op jit(solution)/shard_map/psum | solution.py:145
  578.8 7.6 collective-permute-done.27
  588.0 67.8 %psum.89 = f32[64]{0:T(128)S(1)} all-reduce(f32[64]{0:T(128)S(1)} %multiply_reduce_fusion.5), channel_id=1, replica_groups=mesh['sx'=16,'sy'=8] {'sx','sy'}, use_global_device_ids=true, to_apply=%region_17.18 | all-reduce | flops 64 | bytes 512 | tf_op jit(solution)/shard_map/psum | solution.py:158
  660.5 6.0 all-to-all-start.5
  698.2 7.7 collective-permute-done.31
  707.3 67.3 %psum.90 = f32[64]{0:T(128)S(1)} all-reduce(f32[64]{0:T(128)S(1)} %multiply_reduce_fusion.4), channel_id=1, replica_groups=mesh['sx'=16,'sy'=8] {'sx','sy'}, use_global_device_ids=true, to_apply=%region_19.20 | all-reduce | flops 64 | bytes 512 | tf_op jit(solution)/shard_map/psum | solution.py:145
  795.5 7.7 collective-permute-done.35
  804.7 67.9 %psum.91 = f32[64]{0:T(128)S(1)} all-reduce(f32[64]{0:T(128)S(1)} %multiply_reduce_fusion.3), channel_id=1, replica_groups=mesh['sx'=16,'sy'=8] {'sx','sy'}, use_global_device_ids=true, to_apply=%region_21.22 | all-reduce | flops 64 | bytes 512 | tf_op jit(solution)/shard_map/psum | solution.py:158
  913.4 7.7 collective-permute-done.39
  923.4 67.3 %psum.92 = f32[64]{0:T(128)S(1)} all-reduce(f32[64]{0:T(128)S(1)} %multiply_reduce_fusion.2), channel_id=1, replica_groups=mesh['sx'=16,'sy'=8] {'sx','sy'}, use_global_device_ids=true, to_apply=%region_23.24 | all-reduce | flops 64 | bytes 512 | tf_op jit(solution)/shard_map/psum | solution.py:145
  1012.7 7.7 collective-permute-done.43
  1021.9 67.8 %psum.93 = f32[64]{0:T(128)S(1)} all-reduce(f32[64]{0:T(128)S(1)} %multiply_reduce_fusion.1), channel_id=1, replica_groups=mesh['sx'=16,'sy'=8] {'sx','sy'}, use_global_device_ids=true, to_apply=%region_25.26 | all-reduce | flops 64 | bytes 512 | tf_op jit(solution)/shard_map/psum | solution.py:158
  1130.5 7.7 collective-permute-done.47
  1139.7 67.4 %psum.94 = f32[64]{0:T(128)S(1)} all-reduce(f32[64]{0:T(128)S(1)} %multiply_reduce_fusion), channel_id=1, replica_groups=mesh['sx'=16,'sy'=8] {'sx','sy'}, use_global_device_ids=true, to_apply=%region_27.28 | all-reduce | flops 64 | bytes 512 | tf_op jit(solution)/shard_map/psum | solution.py:145
  1227.9 7.6 collective-permute-done.51
  1237.9 67.8 %psum.95 = f32[64]{0:T(128)S(1)} all-reduce(f32[64]{0:T(128)S(1)} %fusion.48), channel_id=1, replica_groups=mesh['sx'=16,'sy'=8] {'sx','sy'}, use_global_device_ids=true, to_apply=%region_29.30 | all-reduce | flops 64 | bytes 512 | tf_op jit(solution)/shard_map/psum | solution.py:158
  (342 shorter events, 403.4 us)
Async XLA Ops:
  5.6 21.0 %all-to-all-start = ((s32[128,1,4]{2,1,0:T(1,128)}), s32[128,1,4]{2,1,0:T(1,128)S(1)}, u32[]{:S(2)}, u32[]{:S(2)}) async-start(s32[128,1,4]{2,1,0:T(1,128)} %bitcast.7), calls=%async_computation | async-start | bytes 131072 | tf_op jit(solution)/shard_map/all_to_all | solution.py:117
  26.6 14.0 %all-to-all-start.1 = ((bf16[128,2,128]{2,1,0:T(2,128)(2,1)}), bf16[128,2,128]{2,1,0:T(2,128)(2,1)S(1)}, u32[]{:S(2)}, u32[]{:S(2)}) async-start(bf16[128,2,128]{2,1,0:T(2,128)(2,1)} %reshape.1450), calls=%async_computation.1 | async-start | bytes 131072 | tf_op jit(solution)/shard_map/all_to_all | solution.py:110
  53.7 14.6 %collective-permute-start.3 = (bf16[3,1,64,2048]{3,2,1,0:T(8,128)(2,1)S(1)}, bf16[3,1,64,2048]{3,2,1,0:T(8,128)(2,1)S(1)}, u32[]{:S(2)}, u32[]{:S(2)}) collective-permute-start(bf16[3,1,64,2048]{3,2,1,0:T(8,128)(2,1)S(1)} %pad_maximum_fusion), channel_id=1, source_target_pairs={{1,0},{2,1},{3,2},{4,3},{5,4},{6,5},{7,6},{9,8},{10,9},{11,10},{12... | collective-permute-start | bytes 2359304 | tf_op jit(solution)/shard_map/ppermute | solution.py:36
  57.6 11.9 collective-permute-start.2
  73.8 22.1 %all-to-all-start.2 = ((f32[128,1,512]{2,1,0:T(1,128)}), f32[128,1,512]{2,1,0:T(1,128)S(1)}, u32[]{:S(2)}, u32[]{:S(2)}) async-start(f32[128,1,512]{2,1,0:T(1,128)} %reshape.1452), calls=%async_computation.2 | async-start | bytes 524288 | tf_op jit(solution)/shard_map/all_to_all | solution.py:11
  109.9 13.8 %collective-permute-start.7 = (bf16[3,1,64,2048]{3,2,1,0:T(8,128)(2,1)S(1)}, bf16[3,1,64,2048]{3,2,1,0:T(8,128)(2,1)S(1)}, u32[]{:S(2)}, u32[]{:S(2)}) collective-permute-start(bf16[3,1,64,2048]{3,2,1,0:T(8,128)(2,1)S(1)} %pad_maximum_fusion.1), channel_id=1, source_target_pairs={{1,0},{2,1},{3,2},{4,3},{5,4},{6,5},{7,6},{9,8},{10,9},{11,10},{12... | collective-permute-start | bytes 2359304 | tf_op jit(solution)/shard_map/ppermute | solution.py:36
  113.8 11.0 collective-permute-start.6
  139.3 15.3 %collective-permute-start.11 = (bf16[3,1,64,2048]{3,2,1,0:T(8,128)(2,1)S(1)}, bf16[3,1,64,2048]{3,2,1,0:T(8,128)(2,1)S(1)}, u32[]{:S(2)}, u32[]{:S(2)}) collective-permute-start(bf16[3,1,64,2048]{3,2,1,0:T(8,128)(2,1)S(1)} %pad_maximum_fusion.2), channel_id=1, source_target_pairs={{1,0},{2,1},{3,2},{4,3},{5,4},{6,5},{7,6},{9,8},{10,9},{11,10},{12... | collective-permute-start | bytes 2359304 | tf_op jit(solution)/shard_map/ppermute | solution.py:36
  141.2 14.5 %collective-permute-start.10 = (bf16[3,1,64,2048]{3,2,1,0:T(8,128)(2,1)S(1)}, bf16[3,1,64,2048]{3,2,1,0:T(8,128)(2,1)S(1)}, u32[]{:S(2)}, u32[]{:S(2)}) collective-permute-start(bf16[3,1,64,2048]{3,2,1,0:T(8,128)(2,1)S(1)} %pad_maximum_fusion.2), channel_id=1, source_target_pairs={{0,1},{1,2},{2,3},{3,4},{4,5},{5,6},{6,7},{8,9},{9,10},{10,11},{11... | collective-permute-start | bytes 2359304 | tf_op jit(solution)/shard_map/ppermute | solution.py:34
  228.6 16.4 %all-to-all-start.3 = ((f32[128,1,512]{2,1,0:T(1,128)}), f32[128,1,512]{2,1,0:T(1,128)S(1)}, u32[]{:S(2)}, u32[]{:S(2)}) async-start(f32[128,1,512]{2,1,0:T(1,128)} %reshape.1454), calls=%async_computation.3 | async-start | bytes 524288 | tf_op jit(solution)/shard_map/all_to_all | solution.py:11
  258.3 13.8 %collective-permute-start.15 = (bf16[3,1,64,2048]{3,2,1,0:T(8,128)(2,1)S(1)}, bf16[3,1,64,2048]{3,2,1,0:T(8,128)(2,1)S(1)}, u32[]{:S(2)}, u32[]{:S(2)}) collective-permute-start(bf16[3,1,64,2048]{3,2,1,0:T(8,128)(2,1)S(1)} %pad_maximum_fusion.3), channel_id=1, source_target_pairs={{1,0},{2,1},{3,2},{4,3},{5,4},{6,5},{7,6},{9,8},{10,9},{11,10},{12... | collective-permute-start | bytes 2359304 | tf_op jit(solution)/shard_map/ppermute | solution.py:36
  262.2 11.0 collective-permute-start.14
  355.7 13.6 %collective-permute-start.19 = (bf16[3,1,64,2048]{3,2,1,0:T(8,128)(2,1)S(1)}, bf16[3,1,64,2048]{3,2,1,0:T(8,128)(2,1)S(1)}, u32[]{:S(2)}, u32[]{:S(2)}) collective-permute-start(bf16[3,1,64,2048]{3,2,1,0:T(8,128)(2,1)S(1)} %pad_maximum_fusion.4), channel_id=1, source_target_pairs={{1,0},{2,1},{3,2},{4,3},{5,4},{6,5},{7,6},{9,8},{10,9},{11,10},{12... | collective-permute-start | bytes 2359304 | tf_op jit(solution)/shard_map/ppermute | solution.py:36
  359.7 10.8 collective-permute-start.18
  442.3 16.5 %all-to-all-start.4 = ((f32[128,1,512]{2,1,0:T(1,128)}), f32[128,1,512]{2,1,0:T(1,128)S(1)}, u32[]{:S(2)}, u32[]{:S(2)}) async-start(f32[128,1,512]{2,1,0:T(1,128)} %reshape.1456), calls=%async_computation.4 | async-start | bytes 524288 | tf_op jit(solution)/shard_map/all_to_all | solution.py:11
  473.5 13.8 %collective-permute-start.23 = (bf16[3,1,64,2048]{3,2,1,0:T(8,128)(2,1)S(1)}, bf16[3,1,64,2048]{3,2,1,0:T(8,128)(2,1)S(1)}, u32[]{:S(2)}, u32[]{:S(2)}) collective-permute-start(bf16[3,1,64,2048]{3,2,1,0:T(8,128)(2,1)S(1)} %pad_maximum_fusion.5), channel_id=1, source_target_pairs={{1,0},{2,1},{3,2},{4,3},{5,4},{6,5},{7,6},{9,8},{10,9},{11,10},{12... | collective-permute-start | bytes 2359304 | tf_op jit(solution)/shard_map/ppermute | solution.py:36
  477.4 11.0 collective-permute-start.22
  572.7 13.7 %collective-permute-start.27 = (bf16[3,1,64,2048]{3,2,1,0:T(8,128)(2,1)S(1)}, bf16[3,1,64,2048]{3,2,1,0:T(8,128)(2,1)S(1)}, u32[]{:S(2)}, u32[]{:S(2)}) collective-permute-start(bf16[3,1,64,2048]{3,2,1,0:T(8,128)(2,1)S(1)} %pad_maximum_fusion.6), channel_id=1, source_target_pairs={{1,0},{2,1},{3,2},{4,3},{5,4},{6,5},{7,6},{9,8},{10,9},{11,10},{12... | collective-permute-start | bytes 2359304 | tf_op jit(solution)/shard_map/ppermute | solution.py:36
  660.5 16.9 %all-to-all-start.5 = ((f32[128,1,512]{2,1,0:T(1,128)}), f32[128,1,512]{2,1,0:T(1,128)S(1)}, u32[]{:S(2)}, u32[]{:S(2)}) async-start(f32[128,1,512]{2,1,0:T(1,128)} %reshape.1458), calls=%async_computation.5 | async-start | bytes 524288 | tf_op jit(solution)/shard_map/all_to_all | solution.py:11
  692.1 13.8 %collective-permute-start.31 = (bf16[3,1,64,2048]{3,2,1,0:T(8,128)(2,1)S(1)}, bf16[3,1,64,2048]{3,2,1,0:T(8,128)(2,1)S(1)}, u32[]{:S(2)}, u32[]{:S(2)}) collective-permute-start(bf16[3,1,64,2048]{3,2,1,0:T(8,128)(2,1)S(1)} %pad_maximum_fusion.7), channel_id=1, source_target_pairs={{1,0},{2,1},{3,2},{4,3},{5,4},{6,5},{7,6},{9,8},{10,9},{11,10},{12... | collective-permute-start | bytes 2359304 | tf_op jit(solution)/shard_map/ppermute | solution.py:36
  696.0 11.0 collective-permute-start.30
  789.6 13.5 %collective-permute-start.35 = (bf16[3,1,64,2048]{3,2,1,0:T(8,128)(2,1)S(1)}, bf16[3,1,64,2048]{3,2,1,0:T(8,128)(2,1)S(1)}, u32[]{:S(2)}, u32[]{:S(2)}) collective-permute-start(bf16[3,1,64,2048]{3,2,1,0:T(8,128)(2,1)S(1)} %pad_maximum_fusion.8), channel_id=1, source_target_pairs={{1,0},{2,1},{3,2},{4,3},{5,4},{6,5},{7,6},{9,8},{10,9},{11,10},{12... | collective-permute-start | bytes 2359304 | tf_op jit(solution)/shard_map/ppermute | solution.py:36
  793.6 10.8 collective-permute-start.34
  876.2 16.5 %all-to-all-start.6 = ((f32[128,1,512]{2,1,0:T(1,128)}), f32[128,1,512]{2,1,0:T(1,128)S(1)}, u32[]{:S(2)}, u32[]{:S(2)}) async-start(f32[128,1,512]{2,1,0:T(1,128)} %reshape.1460), calls=%async_computation.6 | async-start | bytes 524288 | tf_op jit(solution)/shard_map/all_to_all | solution.py:11
  907.4 13.8 %collective-permute-start.39 = (bf16[3,1,64,2048]{3,2,1,0:T(8,128)(2,1)S(1)}, bf16[3,1,64,2048]{3,2,1,0:T(8,128)(2,1)S(1)}, u32[]{:S(2)}, u32[]{:S(2)}) collective-permute-start(bf16[3,1,64,2048]{3,2,1,0:T(8,128)(2,1)S(1)} %pad_maximum_fusion.9), channel_id=1, source_target_pairs={{1,0},{2,1},{3,2},{4,3},{5,4},{6,5},{7,6},{9,8},{10,9},{11,10},{12... | collective-permute-start | bytes 2359304 | tf_op jit(solution)/shard_map/ppermute | solution.py:36
  911.3 11.0 collective-permute-start.38
  1006.7 13.7 %collective-permute-start.43 = (bf16[3,1,64,2048]{3,2,1,0:T(8,128)(2,1)S(1)}, bf16[3,1,64,2048]{3,2,1,0:T(8,128)(2,1)S(1)}, u32[]{:S(2)}, u32[]{:S(2)}) collective-permute-start(bf16[3,1,64,2048]{3,2,1,0:T(8,128)(2,1)S(1)} %pad_maximum_fusion.10), channel_id=1, source_target_pairs={{1,0},{2,1},{3,2},{4,3},{5,4},{6,5},{7,6},{9,8},{10,9},{11,10},{12... | collective-permute-start | bytes 2359304 | tf_op jit(solution)/shard_map/ppermute | solution.py:36
  1010.7 10.9 collective-permute-start.42
  1093.2 16.6 %all-to-all-start.7 = ((f32[128,1,512]{2,1,0:T(1,128)}), f32[128,1,512]{2,1,0:T(1,128)S(1)}, u32[]{:S(2)}, u32[]{:S(2)}) async-start(f32[128,1,512]{2,1,0:T(1,128)} %reshape.1462), calls=%async_computation.7 | async-start | bytes 524288 | tf_op jit(solution)/shard_map/all_to_all | solution.py:11
  1124.5 13.8 %collective-permute-start.47 = (bf16[3,1,64,2048]{3,2,1,0:T(8,128)(2,1)S(1)}, bf16[3,1,64,2048]{3,2,1,0:T(8,128)(2,1)S(1)}, u32[]{:S(2)}, u32[]{:S(2)}) collective-permute-start(bf16[3,1,64,2048]{3,2,1,0:T(8,128)(2,1)S(1)} %pad_maximum_fusion.11), channel_id=1, source_target_pairs={{1,0},{2,1},{3,2},{4,3},{5,4},{6,5},{7,6},{9,8},{10,9},{11,10},{12... | collective-permute-start | bytes 2359304 | tf_op jit(solution)/shard_map/ppermute | solution.py:36
  1128.4 11.0 collective-permute-start.46
  1221.7 13.7 %collective-permute-start.51 = (bf16[3,1,64,2048]{3,2,1,0:T(8,128)(2,1)S(1)}, bf16[3,1,64,2048]{3,2,1,0:T(8,128)(2,1)S(1)}, u32[]{:S(2)}, u32[]{:S(2)}) collective-permute-start(bf16[3,1,64,2048]{3,2,1,0:T(8,128)(2,1)S(1)} %pad_maximum_fusion.12), channel_id=1, source_target_pairs={{1,0},{2,1},{3,2},{4,3},{5,4},{6,5},{7,6},{9,8},{10,9},{11,10},{12... | collective-permute-start | bytes 2359304 | tf_op jit(solution)/shard_map/ppermute | solution.py:36
  (71 other events, 2774.9 us)
